TPU v7x, 32 devices: a whole 2x2x4 slice. The times are simulated.
32 devices in a mesh: pairs: 8 (over z, x), grp: 4 (over y, core).
Axes of the slice: x: 2, y: 2, z: 4, core: 2. Of those that a mesh axis runs over, the one named last changes fastest.
Arguments:
- coefficients: bfloat16 [128, 512, 128], P('pairs', 'grp'), may hold values from -0.4140625 to 0.4140625
- domain: int32 [128, 512], P('pairs', 'grp'), may hold values from 0 to 767, as said below
- coupling_owner: int32 [128, 8], P('pairs'), may hold values from 0 to 7, all different within a row; in each aligned block of 16 rows (0 to 15, 16 to 31, ...) at most 16 rows name the same one
- coupling_slot: int32 [128, 8], P('pairs'), may hold values from 0 to 15
- coupling_fock: float32 [128, 8], P('pairs'), may hold values from -0.5 to 0.5
- exchange_integrals: float32 [128, 128, 128], P('pairs'), may hold values from -6 to 6
- pno_energy: float32 [128, 128], P('pairs'), may hold values from 0.3 to 3
- pair_shift: float32 [128], P('pairs'), may hold values from 0.4 to 2
- amplitudes_start: float32 [128, 128, 128], P('pairs'), may hold values from -1.8 to 1.8
Outputs:
- amplitudes: float32 [128, 128, 128], P('pairs')
Inputs may be any that keep to these rules, and one draw needn't show every extreme that they name: `coupling_owner`: each row names different indices. Among the 16 rows of one index of pairs no value is named more than 16 times, a bound that some block reaches. `domain`: for each pair and each g from 0 to 3, the entries g * 128 to (g + 1) * 128 - 1 are distinct numbers from g * 192 to (g + 1) * 192 - 1.
All inputs are finite; a program needn't handle non-finite values.
Results may differ from a plain program's by a relative error of at most 0.0025.
Values may be sent and summed in bfloat16 or wider, within the bound.
A program may use at most 128 MiB of HBM per device.

v0:
```python
import jax
import jax.numpy as jnp
from jax import lax
from jax.sharding import PartitionSpec as P

NB = 192
ITERS = 2


def on_device(
    coefficients,
    domain,
    coupling_owner,
    coupling_slot,
    coupling_fock,
    exchange_integrals,
    pno_energy,
    pair_shift,
    amplitudes_start,
):
    pair_count = coefficients.shape[0]
    block_rows = coefficients.shape[1]
    pno_count = coefficients.shape[2]
    link_count = coupling_owner.shape[1]
    pair_ranks = lax.axis_size("pairs")
    capacity = min(pair_count, (pair_count * link_count + pair_ranks - 1) // pair_ranks + 1)
    group_index = lax.axis_index("grp")
    local_dom = domain - group_index * NB
    owners = coupling_owner.T.reshape(-1)
    slots = coupling_slot.T.reshape(-1)
    owner_hits = (owners[:, None] == jnp.arange(pair_ranks, dtype=jnp.int32)[None, :]).astype(
        jnp.int32
    )
    earlier = jnp.cumsum(owner_hits, axis=0) - owner_hits
    link_rank = jnp.sum(earlier * owner_hits, axis=1)
    slot_hits = owner_hits[:, :, None] * (
        link_rank[:, None, None] == jnp.arange(capacity, dtype=jnp.int32)[None, None, :]
    ).astype(jnp.int32)
    request = jnp.sum(slot_hits * slots[:, None, None], axis=0)
    wanted = lax.all_to_all(request, "pairs", split_axis=0, concat_axis=0, tiled=True).reshape(-1)
    position = owners * capacity + link_rank
    outgoing_rows = jnp.take(coefficients, wanted, axis=0).reshape(
        pair_ranks, capacity, block_rows, pno_count
    )
    outgoing_dom = jnp.take(local_dom, wanted, axis=0).reshape(pair_ranks, capacity, block_rows)
    incoming_rows = lax.all_to_all(outgoing_rows, "pairs", split_axis=0, concat_axis=0, tiled=True)
    incoming_dom = lax.all_to_all(outgoing_dom, "pairs", split_axis=0, concat_axis=0, tiled=True)
    source_rows = jnp.take(
        incoming_rows.reshape(pair_ranks * capacity, block_rows, pno_count), position, axis=0
    )
    source_rows = source_rows.reshape(link_count, pair_count, block_rows, pno_count)
    source_dom = jnp.take(incoming_dom.reshape(pair_ranks * capacity, block_rows), position, axis=0)
    source_dom = source_dom.reshape(link_count, pair_count, block_rows)
    match = (local_dom[None, :, :, None] == source_dom[:, :, None, :]).astype(jnp.bfloat16)
    gathered = jnp.einsum(
        "kprs,kpsc->kprc", match, source_rows, preferred_element_type=jnp.float32
    ).astype(jnp.bfloat16)
    position_links = position.reshape(link_count, pair_count)
    fock_links = coupling_fock.T
    intersection = lax.psum(
        jnp.einsum("pra,kprc->kpac", coefficients, gathered, preferred_element_type=jnp.float32),
        "grp",
    )
    intersection_half = intersection.astype(jnp.bfloat16)
    used_links = intersection_half.shape[0]
    denominator = pno_energy[:, :, None] + pno_energy[:, None, :] + pair_shift[:, None, None]
    amplitudes = amplitudes_start
    for iteration in range(ITERS):
        sendable = amplitudes.astype(jnp.bfloat16)
        outgoing_amp = jnp.take(sendable, wanted, axis=0).reshape(
            pair_ranks, capacity, pno_count, pno_count
        )
        incoming_amp = lax.all_to_all(
            outgoing_amp, "pairs", split_axis=0, concat_axis=0, tiled=True
        )
        source_amp = jnp.take(
            incoming_amp.reshape(pair_ranks * capacity, pno_count, pno_count),
            position_links.reshape(-1),
            axis=0,
        )
        source_amp = source_amp.reshape(used_links, pair_count, pno_count, pno_count)
        half_proj = jnp.einsum(
            "kpac,kpcd->kpad", intersection_half, source_amp, preferred_element_type=jnp.float32
        ).astype(jnp.bfloat16)
        projected = jnp.einsum(
            "kpad,kpbd->kpab", half_proj, intersection_half, preferred_element_type=jnp.float32
        )
        coupled = jnp.sum(fock_links[:, :, None, None] * projected, axis=0)
        amplitudes = -(exchange_integrals + coupled) / denominator
    return amplitudes


def solution(mesh):
    placed = (
        P("pairs", "grp", None),
        P("pairs", "grp"),
        P("pairs", None),
        P("pairs", None),
        P("pairs", None),
        P("pairs", None, None),
        P("pairs", None),
        P("pairs"),
        P("pairs", None, None),
    )
    return jax.shard_map(
        on_device, mesh=mesh, in_specs=placed, out_specs=P("pairs", None, None), check_vma=False
    )
```

profile of v0, /device:TPU:0, one launch (start us, length us, event | category | flops | bytes accessed | tf_op | source)
XLA Modules:
  0.0 524.1 jit_solution(13798727091787789117)
XLA Ops:
  0.0 0.0 copy-start
  0.0 0.8 reshape.197
  0.8 0.8 mul.76
  1.6 0.1 fusion.43
  1.7 0.2 reduce_window_sum.11
  1.9 0.2 select_reduce_fusion
  2.1 0.8 multiply_reduce_fusion.2
  2.9 7.3 %all-to-all-start = ((s32[8,1,16]{2,1,0:T(1,128)}), s32[8,1,16]{2,1,0:T(1,128)S(1)}, u32[]{:S(2)}, u32[]{:S(2)}) async-start(s32[8,1,16]{2,1,0:T(1,128)} %bitcast.4), calls=%async_computation | async-start | bytes 8192 | tf_op jit(solution)/shard_map/all_to_all | solution.py:40
  10.2 0.7 broadcast_subtract_fusion
  10.9 1.3 convert_element_type.38
  12.2 4.4 all-to-all-done
  16.6 0.1 reshape.201
  16.8 0.5 broadcast.152
  17.3 0.7 reduce.5
  17.9 0.1 reshape.199
  18.0 0.6 gather_fusion
  18.7 0.7 broadcast_select_fusion.7
  19.4 3.4 all-to-all-start.1
  22.8 3.0 gather_fusion.4
  25.8 0.0 copy-done
  25.8 3.1 gather_fusion.2
  28.8 6.0 %broadcast_select_fusion.3 = (bf16[128,128,128]{2,1,0:T(8,128)(2,1)}, bf16[128,128,128]{2,1,0:T(8,128)(2,1)}) fusion(bf16[128,128,128]{2,1,0:T(8,128)(2,1)} %gather_fusion.4, pred[128]{0:T(512)(128)(4,1)S(1)} %compare_and_fusion.3, bf16[128,128,128]{2,1,0:T(8,128)(2,1)} %gather_fusion.2), kind=kLoop, calls=%fused_computation.24 | loop fusion | flops 4194304 | bytes 16777344 | tf_op jit(solution)/shard_map/jit(_take)/select_n | solution.py:70
  34.8 0.0 all-to-all-done.1
  34.8 97.5 %all_to_all.29 = bf16[8,16,128,128]{3,2,1,0:T(8,128)(2,1)} all-to-all(bf16[8,16,128,128]{3,2,1,0:T(8,128)(2,1)} %bitcast.41), channel_id=1, replica_groups=mesh['pairs'=8,'grp'=4] {'pairs'}, dimensions={0} | all-to-all | bytes 8388608 | tf_op jit(solution)/shard_map/all_to_all | solution.py:46
  132.3 0.0 copy-start.4
  132.3 4.7 all-to-all-start.3
  137.0 0.1 reduce_sum.41
  137.1 0.0 copy-done.4
  137.1 0.1 mul.80
  137.2 0.6 gather_fusion.1
  137.9 0.1 broadcast_select_fusion.6
  138.0 5.2 gather_fusion.3
  143.2 85.8 %all-to-all-done.3 = bf16[8,16,128,128]{3,2,1,0:T(8,128)(2,1)} async-done(((bf16[8,16,128,128]{3,2,1,0:T(8,128)(2,1)}), bf16[8,16,128,128]{3,2,1,0:T(8,128)(2,1)}, u32[]{:S(2)}, u32[]{:S(2)}) %all-to-all-start.3) | async-done | bytes 4194336 | tf_op jit(solution)/shard_map/all_to_all | solution.py:73
  229.1 5.2 %gather_fusion.5 = bf16[128,128,128]{2,1,0:T(8,128)(2,1)} fusion(bf16[128,128,128]{2,1,0:T(8,128)(2,1)} %bitcast.19, s32[1024]{0:T(1024)S(1)} %pad_clamp_fusion), kind=kCustom, calls=%fused_computation.4.clone | custom fusion | bytes 8389120 | tf_op jit(solution)/shard_map/jit(_take)/gather | solution.py:76
  234.3 6.0 %broadcast_select_fusion = (bf16[128,128,128]{2,1,0:T(8,128)(2,1)}, bf16[128,128,128]{2,1,0:T(8,128)(2,1)}) fusion(bf16[128,128,128]{2,1,0:T(8,128)(2,1)} %gather_fusion.5, pred[128]{0:T(512)(128)(4,1)S(1)} %get-tuple-element.6, bf16[128,128,128]{2,1,0:T(8,128)(2,1)} %gather_fusion.3), kind=kLoop, calls=%fused_computation.21 | loop fusion | flops 4194304 | bytes 16777344 | tf_op jit(solution)/shard_map/jit(_take)/select_n | solution.py:76
  240.3 6.5 %fusion.11 = f32[8,16,128,128]{2,3,0,1:T(8,128)} fusion(bf16[8,16,128,128]{3,2,1,0:T(8,128)(2,1)} %bitcast.43, s32[8,16,128]{2,0,1:T(8,128)S(1)} %copy.25, s32[16,128]{1,0:T(8,128)S(1)} %broadcast_subtract_fusion, bf16[16,128,128]{2,1,0:T(8,128)(2,1)S(1)} %copy-done), kind=kOutput, calls=%fused_computation.27 | convolution fusion | flops 1077936128 | bytes 13180928 | tf_op jit(solution)/shard_map/pra,kprc->kpac/dot_general | solution.py:61
  246.8 0.0 copy-start.6
  246.8 146.3 %all-reduce.1 = bf16[8,16,128,128]{2,3,0,1:T(8,128)(2,1)} all-reduce(f32[8,16,128,128]{2,3,0,1:T(8,128)} %fusion.11), channel_id=1, replica_groups=mesh['pairs'=8,'grp'=4] {'grp'}, use_global_device_ids=true, to_apply=%region_3.6 | all-reduce | flops 2097152 | bytes 12582912 | tf_op jit(solution)/shard_map/psum | solution.py:60
  393.1 0.0 copy-done.6
  393.1 0.0 copy-start.2
  393.1 0.0 copy-start.3
  393.1 0.0 copy-start.5
  393.1 7.5 %multiply_reduce_fusion.1 = f32[16,128,128]{2,1,0:T(8,128)S(1)} fusion(f32[8,16]{1,0:T(8,128)S(1)} %bitcast.55, bf16[8,16,128,128]{2,3,0,1:T(8,128)(2,1)} %all-reduce.1, bf16[8,16,128,128]{3,2,1,0:T(8,128)(2,1)} %bitcast.47), kind=kOutput, calls=%fused_computation.9 | convolution fusion | flops 1079771136 | bytes 9437696 | tf_op jit(solution)/shard_map/kpad,kpbd->kpab/dot_general | solution.py:85
  400.6 0.0 copy-done.2
  400.6 0.0 copy-done.3
  400.6 0.0 copy-done.5
  400.6 0.4 divide_convert_fusion
  401.1 3.0 gather_fusion.6
  404.1 2.6 broadcast_select_fusion.4
  406.7 98.7 %all_to_all.30 = bf16[8,16,128,128]{3,2,1,0:T(8,128)(2,1)} all-to-all(bf16[8,16,128,128]{3,2,1,0:T(8,128)(2,1)S(1)} %bitcast.44), channel_id=1, replica_groups=mesh['pairs'=8,'grp'=4] {'pairs'}, dimensions={0} | all-to-all | bytes 8388608 | tf_op jit(solution)/shard_map/all_to_all | solution.py:73
  505.4 5.2 %gather_fusion.7 = bf16[128,128,128]{2,1,0:T(8,128)(2,1)} fusion(bf16[128,128,128]{2,1,0:T(8,128)(2,1)} %bitcast.45, s32[1024]{0:T(1024)S(1)} %pad_clamp_fusion), kind=kCustom, calls=%fused_computation.5.clone | custom fusion | bytes 8389120 | tf_op jit(solution)/shard_map/jit(_take)/gather | solution.py:76
  510.6 4.6 broadcast_select_fusion.1
  515.2 0.0 copy-start.1
  515.2 7.5 %multiply_reduce_fusion = f32[16,128,128]{2,1,0:T(8,128)S(1)} fusion(f32[8,16]{1,0:T(8,128)S(1)} %bitcast.56, bf16[8,16,128,128]{2,3,0,1:T(8,128)(2,1)} %all-reduce.1, bf16[8,16,128,128]{3,2,1,0:T(8,128)(2,1)} %bitcast.48), kind=kOutput, calls=%fused_computation.8 | convolution fusion | flops 1079771136 | bytes 9437696 | tf_op jit(solution)/shard_map/kpad,kpbd->kpab/dot_general | solution.py:85
  522.7 1.4 negate_divide_fusion
  524.1 0.0 copy-done.1
  (15 shorter events, 0.2 us)
Async XLA Ops:
  0.0 25.8 %copy-start = (bf16[16,128,128]{2,1,0:T(8,128)(2,1)S(1)}, bf16[16,128,128]{2,1,0:T(8,128)(2,1)}, u32[]{:S(2)}) copy-start(bf16[16,128,128]{2,1,0:T(8,128)(2,1)} %param.13) | copy-start | bytes 1572868
  2.9 13.7 %all-to-all-start = ((s32[8,1,16]{2,1,0:T(1,128)}), s32[8,1,16]{2,1,0:T(1,128)S(1)}, u32[]{:S(2)}, u32[]{:S(2)}) async-start(s32[8,1,16]{2,1,0:T(1,128)} %bitcast.4), calls=%async_computation | async-start | bytes 8192 | tf_op jit(solution)/shard_map/all_to_all | solution.py:40
  19.4 15.4 %all-to-all-start.1 = ((s32[8,16,128]{2,1,0:T(8,128)}), s32[8,16,128]{2,1,0:T(8,128)S(1)}, u32[]{:S(2)}, u32[]{:S(2)}) async-start(s32[8,16,128]{2,1,0:T(8,128)} %broadcast_select_fusion.7), calls=%async_computation.1 | async-start | bytes 131072 | tf_op jit(solution)/shard_map/all_to_all | solution.py:47
  132.3 4.8 copy-start.4
  132.3 96.7 %all-to-all-start.3 = ((bf16[8,16,128,128]{3,2,1,0:T(8,128)(2,1)}), bf16[8,16,128,128]{3,2,1,0:T(8,128)(2,1)}, u32[]{:S(2)}, u32[]{:S(2)}) async-start(bf16[8,16,128,128]{3,2,1,0:T(8,128)(2,1)} %bitcast.40), calls=%async_computation.3 | async-start | bytes 8388608 | tf_op jit(solution)/shard_map/all_to_all | solution.py:73
  246.8 146.3 %copy-start.6 = (f32[16,8]{0,1:T(8,128)S(1)}, f32[16,8]{0,1:T(8,128)}, u32[]{:S(2)}) copy-start(f32[16,8]{0,1:T(8,128)} %param.17) | copy-start | bytes 1540
  393.1 7.5 %copy-start.2 = (f32[16,128,128]{2,1,0:T(8,128)S(1)}, f32[16,128,128]{2,1,0:T(8,128)}, u32[]{:S(2)}) copy-start(f32[16,128,128]{2,1,0:T(8,128)} %param.18) | copy-start | bytes 3145732
  393.1 7.5 %copy-start.3 = (f32[16,128]{1,0:T(8,128)S(1)}, f32[16,128]{1,0:T(8,128)}, u32[]{:S(2)}) copy-start(f32[16,128]{1,0:T(8,128)} %param.19) | copy-start | bytes 24580
  393.1 7.5 %copy-start.5 = (f32[16]{0:T(128)S(1)}, f32[16]{0:T(128)}, u32[]{:S(2)}) copy-start(f32[16]{0:T(128)} %param.20) | copy-start | bytes 196
  515.2 8.9 %copy-start.1 = (bf16[16,128,128]{2,1,0:T(8,128)(2,1)S(1)}, bf16[16,128,128]{2,1,0:T(8,128)(2,1)}, u32[]{:S(2)}) copy-start(bf16[16,128,128]{2,1,0:T(8,128)(2,1)} %param.13) | copy-start | bytes 1572868
where the time goes:
time: 525 us; the launch traced here: 524 us
  blocking collectives  342 us (65%)
  waiting for transfers between devices  90.2 us (17%)
  local copies, waits for them, and re-layouts  28.6 us (5%)
  other arithmetic  25.8 us (5%)
  matrix products  21.5 us (4%)
  starting transfers between devices  15.3 us (3%)
    psum x1, blocking collectives, on_device(): lax.psum(jnp.einsum('pra,kprc->kpac', coefficients, gathered, preferred_e...  146 us
    all_to_all x1, blocking collectives, on_device(): lax.all_to_all(outgoing_amp, 'pairs', split_axis=0, concat_axis=0, tiled=...  98.7 us
    all_to_all x1, blocking collectives, on_device(): lax.all_to_all(outgoing_rows, 'pairs', split_axis=0, concat_axis=0, tiled...  97.5 us
    all_to_all x1, waiting for transfers between devices, on_device(): lax.all_to_all(outgoing_amp, 'pairs', split_axis=0, concat_axis=0, tiled=...  85.8 us
    dot_general x2, matrix products, on_device(): jnp.einsum('kpad,kpbd->kpab', half_proj, intersection_half, preferred_ele...  15 us
    select_n x2, other arithmetic, on_device(): jnp.take(incoming_amp.reshape(pair_ranks * capacity, pno_count, pno_count...  10.6 us
  transfers between devices with their start and end apart: 3, of which 2 were waited for; matrix products, arithmetic and copies ran while one was open for 4% of the time, Pallas kernels for 0%

commit v1 on v0

--- a/solution.py
+++ b/solution.py
@@ -57,9 +57,14 @@
     ).astype(jnp.bfloat16)
     position_links = position.reshape(link_count, pair_count)
     fock_links = coupling_fock.T
-    intersection = lax.psum(
-        jnp.einsum("pra,kprc->kpac", coefficients, gathered, preferred_element_type=jnp.float32),
-        "grp",
+    intersection = jnp.sum(
+        lax.all_gather(
+            jnp.einsum(
+                "pra,kprc->kpac", coefficients, gathered, preferred_element_type=jnp.float32
+            ),
+            "grp",
+        ),
+        axis=0,
     )
     intersection_half = intersection.astype(jnp.bfloat16)
     used_links = intersection_half.shape[0]

time: 525 us -> 608 us (1.16)
  waiting for transfers between devices: 90.2 us -> 291 us
  blocking collectives: 342 us -> 196 us
  other arithmetic: 25.8 us -> 40.9 us
  between operations: 0.2 us -> 13.6 us
    all_gather x0 -> x1, waiting for transfers between devices: none -> 201 us  [on_device(): lax.all_gather(jnp.einsum('pra,kprc->kpac', coefficients, gathered, prefe...]
    psum x1 -> x0, blocking collectives: 146 us -> none  [on_device(): lax.psum(jnp.einsum('pra,kprc->kpac', coefficients, gathered, preferred_e...]
    reduce_sum x0 -> x1, other arithmetic: none -> 15.2 us  [on_device(): jnp.sum(lax.all_gather(jnp.einsum('pra,kprc->kpac', coefficients, gathere...]
  transfers between devices with their start and end apart: 3 -> 4, of which waited for: 2 -> 3; matrix products, arithmetic and copies ran while one was open for 4% -> 3% of each run, Pallas kernels for 0% -> 0%
where the time goes in v1:
time: 608 us; the launch traced here: 607 us
  waiting for transfers between devices  291 us (48%)
  blocking collectives  196 us (32%)
  other arithmetic  40.9 us (7%)
  local copies, waits for them, and re-layouts  28.6 us (5%)
  matrix products  21.4 us (4%)
  starting transfers between devices  15.5 us (3%)
  between operations  13.6 us (2%)
    all_gather x1, waiting for transfers between devices, on_device(): lax.all_gather(jnp.einsum('pra,kprc->kpac', coefficients, gathered, prefe...  201 us
    all_to_all x1, blocking collectives, on_device(): lax.all_to_all(outgoing_amp, 'pairs', split_axis=0, concat_axis=0, tiled=...  99 us
    all_to_all x1, blocking collectives, on_device(): lax.all_to_all(outgoing_rows, 'pairs', split_axis=0, concat_axis=0, tiled...  97.5 us
    all_to_all x1, waiting for transfers between devices, on_device(): lax.all_to_all(outgoing_amp, 'pairs', split_axis=0, concat_axis=0, tiled=...  85.6 us
    reduce_sum x1, other arithmetic, on_device(): jnp.sum(lax.all_gather(jnp.einsum('pra,kprc->kpac', coefficients, gathere...  15.2 us
    dot_general x2, matrix products, on_device(): jnp.einsum('kpad,kpbd->kpab', half_proj, intersection_half, preferred_ele...  14.9 us
  transfers between devices with their start and end apart: 4, of which 3 were waited for; matrix products, arithmetic and copies ran while one was open for 3% of the time, Pallas kernels for 0%

profile of v1, /device:TPU:0, one launch (start us, length us, event | category | flops | bytes accessed | tf_op | source)
XLA Modules:
  0.0 607.3 jit_solution(4861316663578787842)
XLA Ops:
  6.5 0.0 copy-start
  6.5 0.8 reshape.197
  7.4 0.8 mul.76
  8.1 0.1 fusion.43
  8.3 0.2 reduce_window_sum.11
  8.5 0.2 select_reduce_fusion
  8.7 0.8 multiply_reduce_fusion.2
  9.5 7.3 %all-to-all-start = ((s32[8,1,16]{2,1,0:T(1,128)}), s32[8,1,16]{2,1,0:T(1,128)S(1)}, u32[]{:S(2)}, u32[]{:S(2)}) async-start(s32[8,1,16]{2,1,0:T(1,128)} %bitcast.4), calls=%async_computation | async-start | bytes 8192 | tf_op jit(solution)/shard_map/all_to_all | solution.py:40
  16.8 0.7 broadcast_subtract_fusion
  17.4 1.3 convert_element_type.38
  18.8 4.4 all-to-all-done
  23.2 0.1 reshape.201
  23.3 0.5 broadcast.152
  23.8 0.7 reduce.5
  24.5 0.1 reshape.199
  24.6 0.6 gather_fusion
  25.2 0.7 broadcast_select_fusion.7
  25.9 3.4 all-to-all-start.1
  29.3 3.0 gather_fusion.4
  32.3 0.0 copy-done
  32.3 3.1 gather_fusion.2
  35.4 6.0 broadcast_select_fusion.3
  41.3 0.0 all-to-all-done.1
  41.3 97.5 %all_to_all.29 = bf16[8,16,128,128]{3,2,1,0:T(8,128)(2,1)} all-to-all(bf16[8,16,128,128]{3,2,1,0:T(8,128)(2,1)} %bitcast.43), channel_id=1, replica_groups=mesh['pairs'=8,'grp'=4] {'pairs'}, dimensions={0} | all-to-all | bytes 8388608 | tf_op jit(solution)/shard_map/all_to_all | solution.py:46
  138.9 0.0 copy-start.4
  138.9 4.7 all-to-all-start.3
  143.5 0.2 all-gather.3.cloned.1.call-start
  143.8 0.1 reduce_sum.50
  143.8 0.0 copy-done.4
  143.9 0.1 mul.80
  144.0 0.6 gather_fusion.1
  144.7 0.1 broadcast_select_fusion.6
  144.8 5.2 gather_fusion.3
  150.0 85.6 %all-to-all-done.3 = bf16[8,16,128,128]{3,2,1,0:T(8,128)(2,1)} async-done(((bf16[8,16,128,128]{3,2,1,0:T(8,128)(2,1)}), bf16[8,16,128,128]{3,2,1,0:T(8,128)(2,1)}, u32[]{:S(2)}, u32[]{:S(2)}) %all-to-all-start.3) | async-done | bytes 4194336 | tf_op jit(solution)/shard_map/all_to_all | solution.py:78
  235.6 5.2 gather_fusion.5
  240.8 6.0 broadcast_select_fusion
  246.8 6.5 %fusion.11 = f32[8,16,128,128]{2,3,0,1:T(8,128)} fusion(bf16[8,16,128,128]{3,2,1,0:T(8,128)(2,1)} %bitcast.45, s32[8,16,128]{2,0,1:T(8,128)S(1)} %copy.23, s32[16,128]{1,0:T(8,128)S(1)} %broadcast_subtract_fusion, bf16[16,128,128]{2,1,0:T(8,128)(2,1)S(1)} %copy-done), kind=kOutput, calls=%fused_computation.27 | convolution fusion | flops 1077936128 | bytes 13180928 | tf_op jit(solution)/shard_map/pra,kprc->kpac/dot_general | solution.py:62
  253.3 0.0 all-gather.3.cloned.1.call-update
  253.3 200.7 %all-gather.3.cloned.1.call-done = f32[32,16,128,128]{2,3,0,1:T(8,128)} async-done(((f32[8,16,128,128]{2,3,0,1:T(8,128)}), f32[32,16,128,128]{2,3,0,1:T(8,128)}) %all-gather.3.cloned.1.call-update) | async-done | bytes 33554448 | tf_op jit(solution)/shard_map/all_gather | solution.py:61
  454.0 0.0 copy-start.6
  454.0 15.2 %reduce_sum.53 = bf16[8,16,128,128]{2,3,0,1:T(8,128)(2,1)} reduce(f32[4,8,16,128,128]{3,4,1,0,2:T(8,128)} %bitcast.41, f32[]{:T(128)} %constant.63.clone.1), dimensions={0}, to_apply=%region_3.6 | reduce | flops 6291456 | bytes 37748740 | tf_op jit(solution)/shard_map/reduce_sum | solution.py:60
  469.3 0.0 copy-done.6
  469.3 0.0 copy-start.2
  469.3 0.0 copy-start.3
  469.3 0.0 copy-start.5
  469.3 7.5 %multiply_reduce_fusion.1 = f32[16,128,128]{2,1,0:T(8,128)S(1)} fusion(f32[8,16]{1,0:T(8,128)S(1)} %bitcast.57, bf16[8,16,128,128]{2,3,0,1:T(8,128)(2,1)} %reduce_sum.53, bf16[8,16,128,128]{3,2,1,0:T(8,128)(2,1)} %bitcast.49), kind=kOutput, calls=%fused_computation.9 | convolution fusion | flops 1079771136 | bytes 9437696 | tf_op jit(solution)/shard_map/kpad,kpbd->kpab/dot_general | solution.py:90
  476.8 0.0 copy-done.2
  476.8 0.0 copy-done.3
  476.8 0.0 copy-done.5
  476.8 0.4 divide_convert_fusion
  477.2 3.0 gather_fusion.6
  480.2 2.6 broadcast_select_fusion.4
  482.8 99.0 %all_to_all.30 = bf16[8,16,128,128]{3,2,1,0:T(8,128)(2,1)} all-to-all(bf16[8,16,128,128]{3,2,1,0:T(8,128)(2,1)S(1)} %bitcast.46), channel_id=1, replica_groups=mesh['pairs'=8,'grp'=4] {'pairs'}, dimensions={0} | all-to-all | bytes 8388608 | tf_op jit(solution)/shard_map/all_to_all | solution.py:78
  581.8 5.2 gather_fusion.7
  587.0 4.6 broadcast_select_fusion.1
  591.6 0.0 copy-start.1
  591.6 7.4 %multiply_reduce_fusion = f32[16,128,128]{2,1,0:T(8,128)S(1)} fusion(f32[8,16]{1,0:T(8,128)S(1)} %bitcast.58, bf16[8,16,128,128]{2,3,0,1:T(8,128)(2,1)} %reduce_sum.53, bf16[8,16,128,128]{3,2,1,0:T(8,128)(2,1)} %bitcast.50), kind=kOutput, calls=%fused_computation.8 | convolution fusion | flops 1079771136 | bytes 9437696 | tf_op jit(solution)/shard_map/kpad,kpbd->kpab/dot_general | solution.py:90
  599.1 1.3 negate_divide_fusion
  600.4 0.0 copy-done.1
  (15 shorter events, 0.2 us)
Async XLA Ops:
  6.5 25.8 %copy-start = (bf16[16,128,128]{2,1,0:T(8,128)(2,1)S(1)}, bf16[16,128,128]{2,1,0:T(8,128)(2,1)}, u32[]{:S(2)}) copy-start(bf16[16,128,128]{2,1,0:T(8,128)(2,1)} %param.13) | copy-start | bytes 1572868
  9.5 13.7 %all-to-all-start = ((s32[8,1,16]{2,1,0:T(1,128)}), s32[8,1,16]{2,1,0:T(1,128)S(1)}, u32[]{:S(2)}, u32[]{:S(2)}) async-start(s32[8,1,16]{2,1,0:T(1,128)} %bitcast.4), calls=%async_computation | async-start | bytes 8192 | tf_op jit(solution)/shard_map/all_to_all | solution.py:40
  25.9 15.4 %all-to-all-start.1 = ((s32[8,16,128]{2,1,0:T(8,128)}), s32[8,16,128]{2,1,0:T(8,128)S(1)}, u32[]{:S(2)}, u32[]{:S(2)}) async-start(s32[8,16,128]{2,1,0:T(8,128)} %broadcast_select_fusion.7), calls=%async_computation.1 | async-start | bytes 131072 | tf_op jit(solution)/shard_map/all_to_all | solution.py:47
  138.9 5.0 copy-start.4
  138.9 96.7 %all-to-all-start.3 = ((bf16[8,16,128,128]{3,2,1,0:T(8,128)(2,1)}), bf16[8,16,128,128]{3,2,1,0:T(8,128)(2,1)}, u32[]{:S(2)}, u32[]{:S(2)}) async-start(bf16[8,16,128,128]{3,2,1,0:T(8,128)(2,1)} %bitcast.42), calls=%async_computation.3 | async-start | bytes 8388608 | tf_op jit(solution)/shard_map/all_to_all | solution.py:78
  143.5 310.5 %all-gather.3.cloned.1.call-start = ((), (), s32[]{:S(2)}) async-start(), calls=%async_computation.5 | async-start | bytes 41943040 | tf_op jit(solution)/shard_map/all_gather | solution.py:61
  454.0 15.2 %copy-start.6 = (f32[16,8]{0,1:T(8,128)S(1)}, f32[16,8]{0,1:T(8,128)}, u32[]{:S(2)}) copy-start(f32[16,8]{0,1:T(8,128)} %param.17) | copy-start | bytes 1540
  469.3 7.5 %copy-start.2 = (f32[16,128,128]{2,1,0:T(8,128)S(1)}, f32[16,128,128]{2,1,0:T(8,128)}, u32[]{:S(2)}) copy-start(f32[16,128,128]{2,1,0:T(8,128)} %param.18) | copy-start | bytes 3145732
  469.3 7.5 %copy-start.3 = (f32[16,128]{1,0:T(8,128)S(1)}, f32[16,128]{1,0:T(8,128)}, u32[]{:S(2)}) copy-start(f32[16,128]{1,0:T(8,128)} %param.19) | copy-start | bytes 24580
  469.3 7.5 %copy-start.5 = (f32[16]{0:T(128)S(1)}, f32[16]{0:T(128)}, u32[]{:S(2)}) copy-start(f32[16]{0:T(128)} %param.20) | copy-start | bytes 196
  591.6 8.8 %copy-start.1 = (bf16[16,128,128]{2,1,0:T(8,128)(2,1)S(1)}, bf16[16,128,128]{2,1,0:T(8,128)(2,1)}, u32[]{:S(2)}) copy-start(bf16[16,128,128]{2,1,0:T(8,128)(2,1)} %param.13) | copy-start | bytes 1572868
Sparse Core Ops, SparseCore 0:
  253.4 200.5 all-gather.2
